TPU v7x, 32 devices: a whole 2x2x4 slice. The times are simulated.
32 devices in a mesh: half: 2 (over y), row: 4 (over z), col: 4 (over x, core).
Axes of the slice: x: 2, y: 2, z: 4, core: 2. Of those that a mesh axis runs over, the one named last changes fastest.
Arguments:
- front_init: float32 [10240, 10240], P(('half', 'row'), 'col'), may hold values from -2 to 8, as said below
- child_update: float32 [2, 8192, 8192], P('half', 'row', 'col'), may hold values from -2 to 8, as said below
- child_map: int32 [2, 8192], replicated, may hold values from 0 to 10239, as said below
Outputs:
- factor_front: float32 [10240, 10240], P(('half', 'row'), 'col')
Inputs may be any that keep to these rules, and one draw needn't show every extreme that they name: `child_map`: each child's entries are distinct. Each aligned block of 128 child indices maps onto one whole block of 128 front indices; write b(j) for the front block of child block j. For every r and q below 4, exactly 4 child blocks j with j % 4 == r have b(j) % 4 == q, and these share one value of b(j) % 8. Symmetric in natural order, and front_init minus the identity is positive semidefinite. `child_update`: each child's matrix is symmetric positive semidefinite.
All inputs are finite; a program needn't handle non-finite values.
Results may differ from a plain program's by a relative error of at most 0.0001.
Values sent between devices are 32-bit elements; how exact they have to be, the bound alone decides.
A program may use at most 256 MiB of HBM per device.

v0:
```python
import jax
import jax.numpy as jnp
from jax import lax
from jax.sharding import PartitionSpec as P

BLOCK_EDGE = 128
PANELS = 2
PANEL = 256


def column_order(which_map, source, grid_size, blocks_dev, slot_count):
    local_ids = jnp.arange(blocks_dev)
    targets = which_map[local_ids * grid_size + source] % grid_size
    return jnp.argsort(targets * blocks_dev + local_ids).reshape(grid_size, slot_count)


def row_slots(which_map, source, grid_size, group_count, blocks_dev, slot_count):
    local_ids = jnp.arange(blocks_dev)
    targets = which_map[local_ids * grid_size + source] % group_count
    onehot = targets[None, :] == jnp.arange(group_count)[:, None]
    ranking = jnp.cumsum(onehot.astype(jnp.int32), axis=1)
    matches = onehot[:, None, :] & (
        ranking[:, None, :] == jnp.arange(1, slot_count + 1)[None, :, None]
    )
    slot_index = jnp.sum(matches.astype(jnp.int32) * local_ids[None, None, :], axis=2)
    filled = jnp.any(matches, axis=2)
    return (slot_index, filled)


def on_device(front_init, child_update, child_map):
    grid_size = lax.axis_size("row")
    halves = lax.axis_size("half")
    group_count = halves * grid_size
    my_child = lax.axis_index("half")
    my_row = lax.axis_index("row")
    my_col = lax.axis_index("col")
    my_group = lax.axis_index(("half", "row"))
    child_rows = child_update.shape[1]
    blocks_dev = child_rows // BLOCK_EDGE
    slot_count = blocks_dev // grid_size
    front_rows, front_cols = front_init.shape
    row_blocks = front_rows // BLOCK_EDGE
    block_map = child_map.reshape(2, -1, BLOCK_EDGE)[:, :, 0] // BLOCK_EDGE
    inner_perm = child_map.reshape(2, -1, BLOCK_EDGE) % BLOCK_EDGE
    own_map = block_map[my_child]
    send_order = column_order(own_map, my_col, grid_size, blocks_dev, slot_count).reshape(-1)
    blocks = child_update[0].reshape(child_rows, blocks_dev, BLOCK_EDGE)
    outgoing = jnp.take(blocks, send_order, axis=1).reshape(child_rows, blocks_dev * BLOCK_EDGE)
    incoming = lax.all_to_all(outgoing, "col", split_axis=1, concat_axis=1, tiled=True)
    slot_index, filled = row_slots(own_map, my_row, grid_size, group_count, blocks_dev, slot_count)
    stacked = incoming.reshape(blocks_dev, BLOCK_EDGE, -1)
    packed = jnp.take(stacked, slot_index.reshape(-1), axis=0).reshape(
        group_count, slot_count, BLOCK_EDGE, -1
    )
    packed = jnp.where(filled[:, :, None, None], packed, 0.0).reshape(
        group_count * slot_count * BLOCK_EDGE, -1
    )
    arrived = lax.all_to_all(packed, ("half", "row"), split_axis=0, concat_axis=0, tiled=True)
    arrived = arrived.reshape(halves, grid_size * slot_count * BLOCK_EDGE, -1)
    front_local = front_init
    sources = jnp.arange(grid_size)
    for which_child in range(2):
        which_map = block_map[which_child]
        which_inner = inner_perm[which_child]
        orders = jax.vmap(
            lambda source: column_order(which_map, source, grid_size, blocks_dev, slot_count)
        )(sources)
        col_blocks = (orders[:, my_col, :] * grid_size + sources[:, None]).reshape(-1)
        col_index = (
            (which_map[col_blocks] // grid_size * BLOCK_EDGE)[:, None] + which_inner[col_blocks]
        ).reshape(-1)
        slot_all, fill_all = jax.vmap(
            lambda source: row_slots(
                which_map, source, grid_size, group_count, blocks_dev, slot_count
            )
        )(sources)
        mine_slot = slot_all[:, my_group, :]
        mine_fill = fill_all[:, my_group, :]
        child_blocks = mine_slot * grid_size + sources[:, None]
        target_blocks = which_map[child_blocks]
        row_index = (target_blocks // group_count * BLOCK_EDGE)[:, :, None] + which_inner[
            child_blocks
        ]
        row_index = jnp.where(mine_fill[:, :, None], row_index, front_rows).reshape(-1)
        spread = (
            jnp.zeros((arrived.shape[1], front_cols), jnp.float32)
            .at[:, col_index]
            .set(arrived[which_child])
        )
        front_local = front_local.at[row_index].add(spread, mode="drop")
    row_ids = jnp.arange(front_rows)
    natural_rows = (
        row_ids // BLOCK_EDGE * group_count + my_group
    ) * BLOCK_EDGE + row_ids % BLOCK_EDGE
    col_ids = jnp.arange(front_cols)
    natural_cols = (col_ids // BLOCK_EDGE * grid_size + my_col) * BLOCK_EDGE + col_ids % BLOCK_EDGE
    identity = jnp.eye(PANEL, dtype=jnp.float32)
    for panel_index in range(PANELS):
        panel_start = panel_index * PANEL
        panel_end = panel_start + PANEL
        panel_slab = lax.all_gather(front_local[:, :BLOCK_EDGE], "col", axis=1, tiled=True)[
            :, panel_start:panel_end
        ]
        pieces = []
        for block_part in range(PANEL // BLOCK_EDGE):
            owner_group = (panel_start // BLOCK_EDGE + block_part) % group_count
            pieces.append(jnp.where(my_group == owner_group, panel_slab[:BLOCK_EDGE], 0.0))
        diagonal = lax.psum(jnp.concatenate(pieces, axis=0), ("half", "row"))
        factor = jnp.linalg.cholesky(diagonal)
        inverse = lax.linalg.triangular_solve(factor, identity, left_side=True, lower=True)
        panel_rows = jnp.dot(panel_slab, inverse.T, precision=lax.Precision.HIGHEST)
        panel_rows = jnp.where((natural_rows >= panel_start)[:, None], panel_rows, 0.0)
        everything = lax.all_gather(panel_rows, ("half", "row"), axis=0, tiled=True)
        everything = everything.reshape(halves, grid_size, row_blocks, BLOCK_EDGE, PANEL)
        selected = lax.dynamic_index_in_dim(everything, my_col, axis=1, keepdims=False)
        column_panel = selected.transpose(1, 0, 2, 3).reshape(front_cols, PANEL)
        update = jnp.dot(panel_rows, column_panel.T, precision=lax.Precision.HIGHEST)
        trailing = (natural_rows >= panel_end)[:, None] & (natural_cols >= panel_end)[None, :]
        front_local = jnp.where(trailing, front_local - update, front_local)
        in_panel = (natural_cols >= panel_start) & (natural_cols < panel_end)
        panel_values = jnp.take(
            panel_rows, jnp.clip(natural_cols - panel_start, 0, PANEL - 1), axis=1
        )
        front_local = jnp.where(in_panel[None, :], panel_values, front_local)
        upper_zero = ((natural_rows >= panel_start) & (natural_rows < panel_end))[:, None] & (
            natural_cols >= panel_end
        )[None, :]
        front_local = jnp.where(upper_zero, 0.0, front_local)
    return front_local


def solution(mesh):
    placed = (P(("half", "row"), "col"), P("half", "row", "col"), P())
    return jax.shard_map(
        on_device, mesh=mesh, in_specs=placed, out_specs=P(("half", "row"), "col"), check_vma=False
    )
```

profile of v0, /device:TPU:0, one launch (start us, length us, event | category | flops | bytes accessed | tf_op | source)
XLA Modules:
  0.0 2033.6 jit_solution(14741416370974196072)
XLA Ops:
  20.2 17.6 copy.111
  37.8 17.6 copy.112
  55.4 13.8 gather_fusion.7
  69.2 17.6 copy.113
  106.3 182.7 %all-to-all-done = f32[2048,4,512]{0,2,1:T(8,128)} async-done(((f32[2048,4,512]{0,2,1:T(8,128)}), f32[2048,4,512]{0,2,1:T(8,128)}, u32[]{:S(2)}, u32[]{:S(2)}) %all-to-all-start) | async-done | bytes 16777248 | tf_op jit(solution)/shard_map/all_to_all | solution.py:49
  289.0 14.1 copy.151
  303.1 18.0 copy.142
  321.2 18.8 gather_fusion.8
  340.0 23.1 %fusion = f32[8,512,2048]{2,1,0:T(8,128)} fusion(pred[8,512]{1,0:T(8,128)(4,1)S(1)} %broadcast_bitcast_fusion, pred[8,512]{1,0:T(8,128)(4,1)S(1)} %broadcast_bitcast_fusion.1, f32[8,512,2048]{2,1,0:T(8,128)} %bitcast.166), kind=kLoop, calls=%fused_computation.25 | loop fusion | flops 16777216 | bytes 67117056 | tf_op jit(solution)/shard_map/jit(_where)/select_n | solution.py:55
  384.7 709.6 %all-to-all-done.1 = f32[8,512,2048]{2,1,0:T(8,128)} async-done(((f32[8,512,2048]{2,1,0:T(8,128)}), f32[8,512,2048]{2,1,0:T(8,128)}, u32[]{:S(2)}, u32[]{:S(2)}) %all-to-all-start.1) | async-done | bytes 33554464 | tf_op jit(solution)/shard_map/all_to_all | solution.py:58
  1094.3 21.1 %fusion.91 = (f32[4,512,2048]{2,1,0:T(8,128)}, f32[4,512,2048]{2,1,0:T(8,128)}) fusion(f32[8,512,2048]{2,1,0:T(8,128)} %all-to-all-done.1), kind=kLoop, calls=%fused_computation.286 | loop fusion | bytes 67108864 | tf_op jit(solution)/shard_map/slice | solution.py:88
  1115.4 17.6 copy.143
  1133.0 21.8 %scatter_custom_fusion = f32[2048,2560]{0,1:T(8,128)} fusion(s32[2048]{0:T(1024)S(1)} %bitcast.190, f32[2048,2048]{0,1:T(8,128)} %copy.143, f32[]{:T(128)} %constant.323.clone.1), kind=kCustom, calls=%fused_computation.30 | custom fusion | bytes 37748740 | tf_op jit(solution)/shard_map/scatter | solution.py:88
  1154.9 20.0 copy.117
  1174.8 17.6 copy.146
  1192.4 21.9 %scatter_custom_fusion.2 = f32[2048,2560]{0,1:T(8,128)} fusion(s32[2048]{0:T(1024)S(1)} %bitcast.189, f32[2048,2048]{0,1:T(8,128)} %copy.146, f32[]{:T(128)} %constant.323.clone.1), kind=kCustom, calls=%fused_computation.28 | custom fusion | bytes 37748740 | tf_op jit(solution)/shard_map/scatter | solution.py:88
  1214.3 19.9 copy.125
  1234.3 42.9 %scatter_fusion = f32[1280,2560]{1,0:T(8,128)} fusion(f32[1280,2560]{1,0:T(8,128)} %copy.186, s32[2048]{0:T(1024)S(1)} %bitcast.180, f32[2048,2560]{1,0:T(8,128)} %copy.117), kind=kCustom, calls=%fused_computation.17 | custom fusion | flops 5242880 | bytes 62922752 | tf_op jit(solution)/shard_map/scatter-add | solution.py:90
  1277.2 42.5 %scatter_fusion.1 = f32[1280,2560]{1,0:T(8,128)} fusion(f32[1280,2560]{1,0:T(8,128)} %scatter_fusion, s32[2048]{0:T(1024)S(1)} %bitcast.181, f32[2048,2560]{1,0:T(8,128)} %copy.125), kind=kCustom, calls=%fused_computation.19 | custom fusion | flops 5242880 | bytes 62922752 | tf_op jit(solution)/shard_map/scatter-add | solution.py:90
  1319.7 14.0 copy.126
  1335.7 22.0 %all-gather.5.cloned.1.call-done = f32[1280,512]{0,1:T(8,128)} async-done(((f32[1280,128]{0,1:T(8,128)}), f32[1280,512]{0,1:T(8,128)}) %all-gather.5.cloned.1.call-update) | async-done | bytes 2621456 | tf_op jit(solution)/shard_map/all_gather | solution.py:101
  1359.7 72.0 %all-reduce.4.cloned.1.call-done = f32[256,256]{0,1:T(8,128)} async-done(((f32[256,256]{0,1:T(8,128)}), f32[256,256]{0,1:T(8,128)}) %all-reduce.4.cloned.1.call-update) | async-done | bytes 262160 | tf_op jit(solution)/shard_map/psum | solution.py:108
  1455.8 11.7 cholesky.147
  1474.5 19.7 custom-call.14
  1511.3 138.7 %all-gather.7.cloned.1.call-done = f32[10240,256]{1,0:T(8,128)} async-done(((f32[1280,256]{1,0:T(8,128)}), f32[10240,256]{1,0:T(8,128)}) %all-gather.7.cloned.1.call-update) | async-done | bytes 10485776 | tf_op jit(solution)/shard_map/all_gather | solution.py:113
  1652.3 19.9 fusion.6
  1674.2 23.8 %all-gather.9.cloned.1.call-done = f32[1280,512]{0,1:T(8,128)} async-done(((f32[1280,128]{0,1:T(8,128)}), f32[1280,512]{0,1:T(8,128)}) %all-gather.9.cloned.1.call-update) | async-done | bytes 2621456 | tf_op jit(solution)/shard_map/all_gather | solution.py:101
  1700.2 72.0 %all-reduce.6.cloned.1.call-done = f32[256,256]{0,1:T(8,128)} async-done(((f32[256,256]{0,1:T(8,128)}), f32[256,256]{0,1:T(8,128)}) %all-reduce.6.cloned.1.call-update) | async-done | bytes 262160 | tf_op jit(solution)/shard_map/psum | solution.py:108
  1814.9 19.7 custom-call.16
  1851.9 138.5 %all-gather.11.cloned.1.call-done = f32[10240,256]{1,0:T(8,128)} async-done(((f32[1280,256]{1,0:T(8,128)}), f32[10240,256]{1,0:T(8,128)}) %all-gather.11.cloned.1.call-update) | async-done | bytes 10485776 | tf_op jit(solution)/shard_map/all_gather | solution.py:113
  1992.7 19.9 fusion.8
  2012.6 13.9 copy.137
  (202 shorter events, 180.4 us)
Async XLA Ops:
  6.5 10.8 copy-start.2
  98.4 190.7 %all-to-all-start = ((f32[2048,4,512]{0,2,1:T(8,128)}), f32[2048,4,512]{0,2,1:T(8,128)}, u32[]{:S(2)}, u32[]{:S(2)}) async-start(f32[2048,4,512]{0,2,1:T(8,128)} %bitcast_select_fusion.1), calls=%async_computation | async-start | bytes 33554432 | tf_op jit(solution)/shard_map/all_to_all | solution.py:49
  363.1 731.2 %all-to-all-start.1 = ((f32[8,512,2048]{2,1,0:T(8,128)}), f32[8,512,2048]{2,1,0:T(8,128)}, u32[]{:S(2)}, u32[]{:S(2)}) async-start(f32[8,512,2048]{2,1,0:T(8,128)} %fusion), calls=%async_computation.1 | async-start | bytes 67108864 | tf_op jit(solution)/shard_map/all_to_all | solution.py:58
  370.1 987.6 %all-gather.5.cloned.1.call-start = ((), (), s32[]{:S(2)}) async-start(), calls=%async_computation.2 | async-start | bytes 3276800 | tf_op jit(solution)/shard_map/all_gather | solution.py:101
  1234.3 42.9 %copy-start.3 = (s32[2048,1]{0,1:T(1,128)S(1)}, s32[2048,1]{0,1:T(1,128)}, u32[]{:S(2)}) copy-start(s32[2048,1]{0,1:T(1,128)} %compare_select_fusion.1) | copy-start | bytes 24580
  1335.6 96.0 %all-reduce.4.cloned.1.call-start = ((), (), s32[]{:S(2)}) async-start(), calls=%async_computation.3 | async-start | bytes 524288 | tf_op jit(solution)/shard_map/psum | solution.py:108
  1359.4 290.6 %all-gather.7.cloned.1.call-start = ((), (), s32[]{:S(2)}) async-start(), calls=%async_computation.4 | async-start | bytes 11796480 | tf_op jit(solution)/shard_map/all_gather | solution.py:113
  1499.7 198.3 %all-gather.9.cloned.1.call-start = ((), (), s32[]{:S(2)}) async-start(), calls=%async_computation.5 | async-start | bytes 3276800 | tf_op jit(solution)/shard_map/all_gather | solution.py:101
  1501.6 150.7 %copy-start.1 = (f32[1280,256]{1,0:T(8,128)S(1)}, f32[1280,256]{1,0:T(8,128)}, u32[]{:S(2)}) copy-start(f32[1280,256]{1,0:T(8,128)} %convolution_select_fusion.1) | copy-start | bytes 3932164
  1674.2 98.0 %all-reduce.6.cloned.1.call-start = ((), (), s32[]{:S(2)}) async-start(), calls=%async_computation.6 | async-start | bytes 524288 | tf_op jit(solution)/shard_map/psum | solution.py:108
  1699.8 290.7 %all-gather.11.cloned.1.call-start = ((), (), s32[]{:S(2)}) async-start(), calls=%async_computation.7 | async-start | bytes 11796480 | tf_op jit(solution)/shard_map/all_gather | solution.py:113
  1842.0 150.7 %copy-start = (f32[1280,256]{1,0:T(8,128)S(1)}, f32[1280,256]{1,0:T(8,128)}, u32[]{:S(2)}) copy-start(f32[1280,256]{1,0:T(8,128)} %convolution_select_fusion) | copy-start | bytes 3932164
Sparse Core Ops, SparseCore 0:
  1335.7 21.9 all-gather.4
  1361.1 70.5 all-reduce.3
  1499.9 150.1 all-gather.6
  1674.3 23.7 all-gather.8
  1701.6 70.5 all-reduce.5
  1840.3 150.1 all-gather.10
where the time goes:
time: 2040 us; the launch traced here: 2030 us
  waiting for transfers between devices  1360 us (67%)
  local copies, waits for them, and re-layouts  348 us (17%)
  other arithmetic  242 us (12%)
  matrix products  51.8 us (3%)
    all_to_all x1, waiting for transfers between devices, on_device(): lax.all_to_all(packed, ('half', 'row'), split_axis=0, concat_axis=0, tile...  710 us
    all_gather x2, waiting for transfers between devices, on_device(): everything = lax.all_gather(panel_rows, ('half', 'row'), axis=0, tiled=True)  277 us
    all_to_all x1, waiting for transfers between devices, on_device(): lax.all_to_all(outgoing, 'col', split_axis=1, concat_axis=1, tiled=True)  183 us
    psum x2, waiting for transfers between devices, on_device(): diagonal = lax.psum(jnp.concatenate(pieces, axis=0), ('half', 'row'))  144 us
    scatter-add x2, other arithmetic, on_device(): front_local = front_local.at[row_index].add(spread, mode='drop')  85.4 us
    scatter x4, local copies, waits for them, and re-layouts, on_device(): spread = jnp.zeros((arrived.shape[1], front_cols), jnp.float32).at[:, col...  83.6 us
    another operation x14, other arithmetic, on_device(): factor = jnp.linalg.cholesky(diagonal)  69.3 us
    slice x3, local copies, waits for them, and re-layouts, on_device(): arrived[which_child]  56.4 us
  transfers between devices with their start and end apart: 8, of which 8 were waited for; matrix products, arithmetic and copies ran while one was open for 2% of the time, Pallas kernels for 0%

commit v1 on v0

--- a/solution.py
+++ b/solution.py
@@ -105,7 +105,7 @@
         for block_part in range(PANEL // BLOCK_EDGE):
             owner_group = (panel_start // BLOCK_EDGE + block_part) % group_count
             pieces.append(jnp.where(my_group == owner_group, panel_slab[:BLOCK_EDGE], 0.0))
-        diagonal = lax.psum(jnp.concatenate(pieces, axis=0), ("half", "row"))
+        diagonal = jnp.sum(lax.all_gather(jnp.concatenate(pieces, axis=0), ("half", "row")), axis=0)
         factor = jnp.linalg.cholesky(diagonal)
         inverse = lax.linalg.triangular_solve(factor, identity, left_side=True, lower=True)
         panel_rows = jnp.dot(panel_slab, inverse.T, precision=lax.Precision.HIGHEST)

time: 2040 us -> 1970 us (0.966)
  waiting for transfers between devices: 1360 us -> 1280 us
    psum x2 -> x0, waiting for transfers between devices: 144 us -> none  [on_device(): diagonal = lax.psum(jnp.concatenate(pieces, axis=0), ('half', 'row'))]
    all_gather x0 -> x2, waiting for transfers between devices: none -> 98.6 us  [on_device(): lax.all_gather(jnp.concatenate(pieces, axis=0), ('half', 'row'))]
    all_gather x2, waiting for transfers between devices: 277 us -> 247 us  [on_device(): everything = lax.all_gather(panel_rows, ('half', 'row'), axis=0, tiled=True)]
    gather x2 -> x4, local copies, waits for them, and re-layouts: 19.6 us -> 47.9 us  [on_device(): jnp.take(panel_rows, jnp.clip(natural_cols - panel_start, 0, PANEL - 1),...]
  transfers between devices with their start and end apart: 8 -> 8, of which waited for: 8 -> 8; matrix products, arithmetic and copies ran while one was open for 2% -> 3% of each run, Pallas kernels for 0% -> 0%
where the time goes in v1:
time: 1970 us; the launch traced here: 1960 us
  waiting for transfers between devices  1280 us (65%)
  local copies, waits for them, and re-layouts  346 us (18%)
  other arithmetic  244 us (12%)
  matrix products  51.3 us (3%)
    all_to_all x1, waiting for transfers between devices, on_device(): lax.all_to_all(packed, ('half', 'row'), split_axis=0, concat_axis=0, tile...  710 us
    all_gather x2, waiting for transfers between devices, on_device(): everything = lax.all_gather(panel_rows, ('half', 'row'), axis=0, tiled=True)  247 us
    all_to_all x1, waiting for transfers between devices, on_device(): lax.all_to_all(outgoing, 'col', split_axis=1, concat_axis=1, tiled=True)  183 us
    all_gather x2, waiting for transfers between devices, on_device(): lax.all_gather(jnp.concatenate(pieces, axis=0), ('half', 'row'))  98.6 us
    scatter-add x2, other arithmetic, on_device(): front_local = front_local.at[row_index].add(spread, mode='drop')  85.4 us
    scatter x4, local copies, waits for them, and re-layouts, on_device(): spread = jnp.zeros((arrived.shape[1], front_cols), jnp.float32).at[:, col...  83.6 us
    another operation x14, other arithmetic, on_device(): factor = jnp.linalg.cholesky(diagonal)  69.3 us
    slice x3, local copies, waits for them, and re-layouts, on_device(): arrived[which_child]  56.4 us
  transfers between devices with their start and end apart: 8, of which 8 were waited for; matrix products, arithmetic and copies ran while one was open for 3% of the time, Pallas kernels for 0%

profile of v1, /device:TPU:0, one launch (start us, length us, event | category | flops | bytes accessed | tf_op | source)
XLA Modules:
  0.0 1958.5 jit_solution(4318899226410002754)
XLA Ops:
  20.2 17.6 copy.125
  37.8 17.6 copy.126
  55.4 13.8 gather_fusion.7
  69.2 17.6 copy.127
  106.3 182.7 %all-to-all-done = f32[2048,4,512]{0,2,1:T(8,128)} async-done(((f32[2048,4,512]{0,2,1:T(8,128)}), f32[2048,4,512]{0,2,1:T(8,128)}, u32[]{:S(2)}, u32[]{:S(2)}) %all-to-all-start) | async-done | bytes 16777248 | tf_op jit(solution)/shard_map/all_to_all | solution.py:49
  289.0 14.1 copy.159
  303.1 18.0 copy.150
  321.2 18.8 gather_fusion.8
  340.0 23.1 %fusion = f32[8,512,2048]{2,1,0:T(8,128)} fusion(pred[8,512]{1,0:T(8,128)(4,1)S(1)} %broadcast_bitcast_fusion, pred[8,512]{1,0:T(8,128)(4,1)S(1)} %broadcast_bitcast_fusion.1, f32[8,512,2048]{2,1,0:T(8,128)} %bitcast.168), kind=kLoop, calls=%fused_computation.25 | loop fusion | flops 16777216 | bytes 67117056 | tf_op jit(solution)/shard_map/jit(_where)/select_n | solution.py:55
  384.7 709.6 %all-to-all-done.1 = f32[8,512,2048]{2,1,0:T(8,128)} async-done(((f32[8,512,2048]{2,1,0:T(8,128)}), f32[8,512,2048]{2,1,0:T(8,128)}, u32[]{:S(2)}, u32[]{:S(2)}) %all-to-all-start.1) | async-done | bytes 33554464 | tf_op jit(solution)/shard_map/all_to_all | solution.py:58
  1094.3 21.1 %fusion.91 = (f32[4,512,2048]{2,1,0:T(8,128)}, f32[4,512,2048]{2,1,0:T(8,128)}) fusion(f32[8,512,2048]{2,1,0:T(8,128)} %all-to-all-done.1), kind=kLoop, calls=%fused_computation.286 | loop fusion | bytes 67108864 | tf_op jit(solution)/shard_map/slice | solution.py:88
  1115.4 17.6 copy.151
  1133.0 21.8 %scatter_custom_fusion = f32[2048,2560]{0,1:T(8,128)} fusion(s32[2048]{0:T(1024)S(1)} %bitcast.194, f32[2048,2048]{0,1:T(8,128)} %copy.151, f32[]{:T(128)} %constant.323.clone.1), kind=kCustom, calls=%fused_computation.30 | custom fusion | bytes 37748740 | tf_op jit(solution)/shard_map/scatter | solution.py:88
  1154.9 20.0 %copy.131 = f32[2048,2560]{1,0:T(8,128)} copy(f32[2048,2560]{0,1:T(8,128)} %scatter_custom_fusion) | data formatting | bytes 41943040 | tf_op jit(solution)/shard_map/scatter | solution.py:88
  1174.8 17.6 copy.154
  1192.4 21.9 %scatter_custom_fusion.2 = f32[2048,2560]{0,1:T(8,128)} fusion(s32[2048]{0:T(1024)S(1)} %bitcast.193, f32[2048,2048]{0,1:T(8,128)} %copy.154, f32[]{:T(128)} %constant.323.clone.1), kind=kCustom, calls=%fused_computation.28 | custom fusion | bytes 37748740 | tf_op jit(solution)/shard_map/scatter | solution.py:88
  1214.3 19.9 %copy.139 = f32[2048,2560]{1,0:T(8,128)} copy(f32[2048,2560]{0,1:T(8,128)} %scatter_custom_fusion.2) | data formatting | bytes 41943040 | tf_op jit(solution)/shard_map/scatter | solution.py:88
  1234.3 42.9 %scatter_fusion = f32[1280,2560]{1,0:T(8,128)} fusion(f32[1280,2560]{1,0:T(8,128)} %copy.194, s32[2048]{0:T(1024)S(1)} %bitcast.184, f32[2048,2560]{1,0:T(8,128)} %copy.131), kind=kCustom, calls=%fused_computation.17 | custom fusion | flops 5242880 | bytes 62922752 | tf_op jit(solution)/shard_map/scatter-add | solution.py:90
  1277.2 42.5 %scatter_fusion.1 = f32[1280,2560]{1,0:T(8,128)} fusion(f32[1280,2560]{1,0:T(8,128)} %scatter_fusion, s32[2048]{0:T(1024)S(1)} %bitcast.185, f32[2048,2560]{1,0:T(8,128)} %copy.139), kind=kCustom, calls=%fused_computation.19 | custom fusion | flops 5242880 | bytes 62922752 | tf_op jit(solution)/shard_map/scatter-add | solution.py:90
  1321.7 22.4 %all-gather.9.cloned.1.call-done = f32[1280,512]{1,0:T(8,128)} async-done(((f32[1280,128]{1,0:T(8,128)}), f32[1280,512]{1,0:T(8,128)}) %all-gather.9.cloned.1.call-update) | async-done | bytes 2621456 | tf_op jit(solution)/shard_map/all_gather | solution.py:101
  1346.0 49.5 %all-gather.17.cloned.1.call-done = f32[2048,256]{1,0:T(8,128)} async-done(((f32[256,256]{1,0:T(8,128)}), f32[2048,256]{1,0:T(8,128)}) %all-gather.17.cloned.1.call-update) | async-done | bytes 2097168 | tf_op jit(solution)/shard_map/all_gather | solution.py:108
  1419.5 11.7 cholesky.147
  1438.2 19.7 %custom-call.14 = f32[2,128,128]{1,2,0:T(8,128)S(1)} custom-call(f32[2,128,128]{2,1,0:T(8,128)S(1)} %get-tuple-element.28), custom_call_target="InvertDiagBlocksLowerTriangular" | custom-call | tf_op jit(solution)/shard_map/triangular_solve/custom-call.0 | solution.py:110
  1474.2 14.1 copy.142
  1488.3 123.7 %all-gather.11.cloned.1.call-done = f32[10240,256]{1,0:T(8,128)} async-done(((f32[1280,256]{1,0:T(8,128)}), f32[10240,256]{1,0:T(8,128)}) %all-gather.11.cloned.1.call-update) | async-done | bytes 10485776 | tf_op jit(solution)/shard_map/all_gather | solution.py:113
  1614.1 20.7 %fusion.6 = f32[1280,2560]{1,0:T(8,128)} fusion(f32[1280,2560]{1,0:T(8,128)} %scatter_fusion.1, f32[1280,256]{1,0:T(8,128)S(1)} %copy-done.1, f32[2560,256]{1,0:T(8,128)S(1)} %bitcast.176, f32[2560,1280]{0,1:T(8,128)} %copy.142, pred[2560]{0:T(1024)(128)(4,1)S(1)} %get-tuple-element.97, pred[2560]{0:T(1024)(128)(4,1)S(1)} %get-tuple-element.98, ...), kind=kOutput, calls=%fused_computation.34 | convolution fusion | flops 10089267200 | bytes 43264000 | tf_op jit(solution)/shard_map/dot_general | solution.py:117
  1636.8 24.2 %all-gather.13.cloned.1.call-done = f32[1280,512]{1,0:T(8,128)} async-done(((f32[1280,128]{1,0:T(8,128)}), f32[1280,512]{1,0:T(8,128)}) %all-gather.13.cloned.1.call-update) | async-done | bytes 2621456 | tf_op jit(solution)/shard_map/all_gather | solution.py:101
  1663.1 49.2 %all-gather.19.cloned.1.call-done = f32[2048,256]{1,0:T(8,128)} async-done(((f32[256,256]{1,0:T(8,128)}), f32[2048,256]{1,0:T(8,128)}) %all-gather.19.cloned.1.call-update) | async-done | bytes 2097168 | tf_op jit(solution)/shard_map/all_gather | solution.py:108
  1754.8 19.7 %custom-call.16 = f32[2,128,128]{1,2,0:T(8,128)S(1)} custom-call(f32[2,128,128]{2,1,0:T(8,128)S(1)} %get-tuple-element.29), custom_call_target="InvertDiagBlocksLowerTriangular" | custom-call | tf_op jit(solution)/shard_map/triangular_solve/custom-call.0 | solution.py:110
  1790.8 14.1 copy.146
  1804.9 123.7 %all-gather.15.cloned.1.call-done = f32[10240,256]{1,0:T(8,128)} async-done(((f32[1280,256]{1,0:T(8,128)}), f32[10240,256]{1,0:T(8,128)}) %all-gather.15.cloned.1.call-update) | async-done | bytes 10485776 | tf_op jit(solution)/shard_map/all_gather | solution.py:113
  1930.8 20.7 %fusion.8 = f32[1280,2560]{1,0:T(8,128)} fusion(f32[1280,2560]{1,0:T(8,128)} %fusion.6, f32[1280,256]{1,0:T(8,128)S(1)} %copy-done, f32[2560,256]{1,0:T(8,128)S(1)} %bitcast.175, f32[2560,1280]{0,1:T(8,128)} %copy.146, pred[2560]{0:T(1024)(128)(4,1)S(1)} %get-tuple-element.95, pred[2560]{0:T(1024)(128)(4,1)S(1)} %get-tuple-element.96, ...), kind=kOutput, calls=%fused_computation.36 | convolution fusion | flops 10089267200 | bytes 43264000 | tf_op jit(solution)/shard_map/dot_general | solution.py:117
  (204 shorter events, 178.0 us)
Async XLA Ops:
  6.5 10.8 copy-start.2
  98.4 190.7 %all-to-all-start = ((f32[2048,4,512]{0,2,1:T(8,128)}), f32[2048,4,512]{0,2,1:T(8,128)}, u32[]{:S(2)}, u32[]{:S(2)}) async-start(f32[2048,4,512]{0,2,1:T(8,128)} %bitcast_select_fusion.1), calls=%async_computation | async-start | bytes 33554432 | tf_op jit(solution)/shard_map/all_to_all | solution.py:49
  363.1 731.2 %all-to-all-start.1 = ((f32[8,512,2048]{2,1,0:T(8,128)}), f32[8,512,2048]{2,1,0:T(8,128)}, u32[]{:S(2)}, u32[]{:S(2)}) async-start(f32[8,512,2048]{2,1,0:T(8,128)} %fusion), calls=%async_computation.1 | async-start | bytes 67108864 | tf_op jit(solution)/shard_map/all_to_all | solution.py:58
  370.1 973.9 %all-gather.9.cloned.1.call-start = ((), (), s32[]{:S(2)}) async-start(), calls=%async_computation.2 | async-start | bytes 3276800 | tf_op jit(solution)/shard_map/all_gather | solution.py:101
  1234.3 42.9 %copy-start.3 = (s32[2048,1]{0,1:T(1,128)S(1)}, s32[2048,1]{0,1:T(1,128)}, u32[]{:S(2)}) copy-start(s32[2048,1]{0,1:T(1,128)} %compare_select_fusion.1) | copy-start | bytes 24580
  1321.7 73.9 %all-gather.17.cloned.1.call-start = ((), (), s32[]{:S(2)}) async-start(), calls=%async_computation.6 | async-start | bytes 2359296 | tf_op jit(solution)/shard_map/all_gather | solution.py:108
  1345.8 266.2 %all-gather.11.cloned.1.call-start = ((), (), s32[]{:S(2)}) async-start(), calls=%async_computation.3 | async-start | bytes 11796480 | tf_op jit(solution)/shard_map/all_gather | solution.py:113
  1462.4 198.6 %all-gather.13.cloned.1.call-start = ((), (), s32[]{:S(2)}) async-start(), calls=%async_computation.4 | async-start | bytes 3276800 | tf_op jit(solution)/shard_map/all_gather | solution.py:101
  1474.2 140.0 %copy-start.1 = (f32[1280,256]{1,0:T(8,128)S(1)}, f32[1280,256]{1,0:T(8,128)}, u32[]{:S(2)}) copy-start(f32[1280,256]{1,0:T(8,128)} %convolution_select_fusion.1) | copy-start | bytes 3932164
  1636.8 75.5 %all-gather.19.cloned.1.call-start = ((), (), s32[]{:S(2)}) async-start(), calls=%async_computation.7 | async-start | bytes 2359296 | tf_op jit(solution)/shard_map/all_gather | solution.py:108
  1662.7 265.9 %all-gather.15.cloned.1.call-start = ((), (), s32[]{:S(2)}) async-start(), calls=%async_computation.5 | async-start | bytes 11796480 | tf_op jit(solution)/shard_map/all_gather | solution.py:113
  1790.8 140.0 %copy-start = (f32[1280,256]{1,0:T(8,128)S(1)}, f32[1280,256]{1,0:T(8,128)}, u32[]{:S(2)}) copy-start(f32[1280,256]{1,0:T(8,128)} %convolution_select_fusion) | copy-start | bytes 3932164
Sparse Core Ops, SparseCore 0:
  1321.8 22.2 all-gather.8
  1346.2 49.2 all-gather.16
  1462.5 149.3 all-gather.10
  1636.9 24.0 all-gather.12
  1663.0 49.2 all-gather.18
  1779.2 149.3 all-gather.14
